TPU v7x, 32 devices: a whole 2x2x4 slice. The times are simulated.
32 devices in a mesh: dp: 1, context: 16 (over z, y, x), tensor: 2 (over core).
Axes of the slice: x: 2, y: 2, z: 4, core: 2. Of those that a mesh axis runs over, the one named last changes fastest.
Arguments:
- queries: bfloat16 [1, 2048, 4096], P('dp', 'context', 'tensor'), may hold values from -30 to 30
- keys: bfloat16 [1, 2048, 256], P('dp', 'context', 'tensor'), may hold values from -4 to 4
- values: bfloat16 [1, 2048, 256], P('dp', 'context', 'tensor'), may hold values from -6 to 6
- outputs: bfloat16 [1, 2048, 4096], P('dp', 'context', 'tensor'), may hold values from -6 to 6
- grad_out: bfloat16 [1, 2048, 4096], P('dp', 'context', 'tensor'), may hold values from -24 to 24
- inputs: bfloat16 [1, 2048, 16384], P('dp', ('context', 'tensor')), may hold values from -1.5 to 1.5
- block_doc: int32 [1, 16], P('dp'), may hold values from 0 to 3, never falling along the last dimension, each value on 1 to 8 neighbouring positions
- span_slots: int32 [32], replicated, may hold values from 0 to 31, as said below
Outputs:
- grad_queries: bfloat16 [1, 2048, 4096], P('dp', 'context', 'tensor')
- grad_key_weight: float32 [16384, 256], P('context', 'tensor')
- grad_value_weight: float32 [16384, 256], P('context', 'tensor')
Inputs may be any that keep to these rules, and one draw needn't show every extreme that they name: span_slots is a permutation; slots 2 d and 2 d + 1 hold two spans c and 31 - c.
All inputs are finite; a program needn't handle non-finite values.
Results may differ from a plain program's by a relative error of at most 0.0065.
Values may be sent and summed in bfloat16 or wider, within the bound.
No kernel may reach another device: no remote copies, remote signals or barrier semaphores. Data moves between devices by JAX's collectives and lax.ppermute only.
A program may use at most 64 MiB of HBM per device.

v0:
```python
import math
import jax
import jax.numpy as jnp
from jax import lax
from jax.sharding import PartitionSpec as P


def table_lookup(entries, positions):
    matches = positions[..., None] == jnp.arange(entries.shape[-1], dtype=jnp.int32)
    return jnp.sum(jnp.where(matches, entries, 0), axis=-1)


def on_device(queries, keys, values, outputs, grad_out, inputs, block_doc, span_slots):
    batch_count, row_count, query_width = queries.shape
    head_size = keys.shape[2]
    group_size = query_width // head_size
    slot_count = span_slots.shape[0]
    span_rows = row_count // 2
    total_rows = span_rows * slot_count
    block_tokens = total_rows // block_doc.shape[1]
    key_block = min(512, total_rows)
    block_count = total_rows // key_block
    scaling = 1.0 / math.sqrt(head_size)
    my_index = lax.axis_index("context")
    offsets = jnp.arange(row_count, dtype=jnp.int32)
    query_position = (
        table_lookup(span_slots, 2 * my_index + offsets // span_rows) * span_rows
        + offsets % span_rows
    )
    query_document = table_lookup(block_doc[:, None, :], (query_position // block_tokens)[None, :])
    key_document = jnp.repeat(block_doc, block_tokens, axis=1)
    slot_index = jnp.arange(slot_count, dtype=jnp.int32)
    inverse = jnp.sum(
        jnp.where(span_slots[None, :] == slot_index[:, None], slot_index[None, :], 0), axis=1
    )
    gathered_keys, gathered_values = (
        lax.all_gather(keys, "context", axis=1, tiled=True),
        lax.all_gather(values, "context", axis=1, tiled=True),
    )
    key_rows = gathered_keys.reshape(batch_count, slot_count, span_rows, head_size)[
        :, inverse
    ].reshape(batch_count, total_rows, head_size)
    value_rows = gathered_values.reshape(batch_count, slot_count, span_rows, head_size)[
        :, inverse
    ].reshape(batch_count, total_rows, head_size)
    query_head_rows = queries.reshape(batch_count, row_count, group_size, head_size)
    gradient_heads = grad_out.reshape(batch_count, row_count, group_size, head_size)
    output_heads = outputs.reshape(batch_count, row_count, group_size, head_size)
    row_delta = jnp.einsum(
        "bqgd,bqgd->bgq", gradient_heads, output_heads, preferred_element_type=jnp.float32
    )[..., None]

    def block_mask(block_start):
        key_position = block_start + jnp.arange(key_block, dtype=jnp.int32)
        key_portion = lax.dynamic_slice_in_dim(key_document, block_start, key_block, 1)
        causal = key_position[None, None, :] <= query_position[None, :, None]
        same_document = key_portion[:, None, :] == query_document[:, :, None]
        return (causal & same_document)[:, None]

    def block_scores(key_portion):
        return (
            jnp.einsum(
                "xztw,xjw->xtzj", query_head_rows, key_portion, preferred_element_type=jnp.float32
            )
            * scaling
        )

    def first_pass(state, block_number):
        block_start = block_number * key_block
        allowed = block_mask(block_start)
        running_max, running_sum = state
        key_portion = lax.dynamic_slice_in_dim(key_rows, block_start, key_block, 1)
        scores = block_scores(key_portion)
        new_max = jnp.maximum(running_max, jnp.max(jnp.where(allowed, scores, -1e30), axis=3))
        weights = jnp.where(allowed, jnp.exp(scores - new_max[..., None]), 0.0)
        return (
            (new_max, running_sum * jnp.exp(running_max - new_max) + jnp.sum(weights, axis=3)),
            None,
        )

    start_max = jnp.full((batch_count, group_size, row_count), -1e30, jnp.float32)
    (running_max, running_sum), unused = lax.scan(
        first_pass, (start_max, jnp.zeros_like(start_max)), jnp.arange(block_count)
    )
    log_norm = (running_max + jnp.log(running_sum))[..., None]

    def second_pass(query_grad, block_number):
        block_start = block_number * key_block
        allowed = block_mask(block_start)
        carried = query_grad
        key_portion = lax.dynamic_slice_in_dim(key_rows, block_start, key_block, 1)
        value_portion = lax.dynamic_slice_in_dim(value_rows, block_start, key_block, 1)
        scores = block_scores(key_portion)
        attention = jnp.where(allowed, jnp.exp(scores - log_norm), 0.0)
        attention_lowered = attention.astype(jnp.bfloat16)
        value_grad = jnp.einsum(
            "elcj,ecla->eja", attention_lowered, gradient_heads, preferred_element_type=jnp.float32
        )
        attention_grad = jnp.einsum(
            "xztw,xjw->xtzj", gradient_heads, value_portion, preferred_element_type=jnp.float32
        )
        score_gradient = (attention * (attention_grad - row_delta)).astype(jnp.bfloat16)
        carried = carried + jnp.einsum(
            "lseu,luv->lesv", score_gradient, key_portion, preferred_element_type=jnp.float32
        )
        key_grad = (
            jnp.einsum(
                "elcj,ecla->eja",
                score_gradient,
                query_head_rows,
                preferred_element_type=jnp.float32,
            )
            * scaling
        )
        return (carried, jnp.concatenate([key_grad, value_grad], axis=2))

    start_grad = jnp.zeros((batch_count, row_count, group_size, head_size), jnp.float32)
    query_grad, block_grads = lax.scan(second_pass, start_grad, jnp.arange(block_count))
    grad_queries = (
        (query_grad * scaling).astype(jnp.bfloat16).reshape(batch_count, row_count, query_width)
    )
    position_grads = jnp.moveaxis(block_grads, 0, 1).reshape(
        batch_count, slot_count, span_rows, 2 * head_size
    )
    stored_grads = position_grads[:, span_slots].reshape(batch_count, total_rows, 2 * head_size)
    local_grads = lax.psum_scatter(stored_grads, "context", scatter_dimension=1, tiled=True)
    grads_low = local_grads.astype(jnp.bfloat16)
    token_rows = lax.all_gather(inputs, "tensor", axis=1, tiled=True)
    shares = lax.psum_scatter(
        jnp.einsum("bnd,bne->de", token_rows, grads_low, preferred_element_type=jnp.float32),
        "context",
        scatter_dimension=0,
        tiled=True,
    )
    summed = lax.psum(shares, "dp")
    return (grad_queries, summed[:, :head_size], summed[:, head_size:])


def solution(mesh):
    in_specs = (
        P("dp", "context", "tensor"),
        P("dp", "context", "tensor"),
        P("dp", "context", "tensor"),
        P("dp", "context", "tensor"),
        P("dp", "context", "tensor"),
        P("dp", ("context", "tensor"), None),
        P("dp", None),
        P(),
    )
    out_specs = (P("dp", "context", "tensor"), P("context", "tensor"), P("context", "tensor"))
    return jax.shard_map(
        on_device, mesh=mesh, in_specs=in_specs, out_specs=out_specs, check_vma=False
    )
```

profile of v0, /device:TPU:10, one launch (start us, length us, event | category | flops | bytes accessed | tf_op | source)
XLA Modules:
  0.0 596.3 jit_solution(16975515604377176983)
XLA Ops:
  8.1 0.7 all-gather.2.cloned.1.call-update
  8.9 0.8 select_reduce_fusion.1
  9.6 0.7 select_reduce_fusion
  10.4 1.3 copy.42
  11.7 0.3 copy.43
  12.0 33.0 %all_gather.9 = bf16[1,2048,128]{2,1,0:T(8,128)(2,1)S(1)} all-gather(bf16[1,128,128]{2,1,0:T(8,128)(2,1)S(1)} %copy-done.2), channel_id=1, replica_groups=mesh['dp'=1,'context'=16,'tensor'=2] {'context'}, dimensions={1}, use_global_device_ids=true | all-gather | bytes 557056 | tf_op jit(solution)/shard_map/all_gather | solution.py:37
  45.1 0.6 gather_fusion
  45.8 12.6 %while.26 = (s32[]{:T(128)}, f32[1,16,128]{2,1,0:T(8,128)S(1)}, f32[1,16,128]{2,1,0:T(8,128)S(1)}, s32[4]{0:T(128)S(1)}, s32[128]{0:T(128)S(1)}, /*index=5*/s32[...) while((s32[]{:T(128)}, f32[1,16,128]{2,1,0:T(8,128)S(1)}, ...), condition=%wide.region_6.7_spmd.clone, body=%wide.region_3.6_spmd.clone.sunk | while | flops 275982848 | bytes 9358550 | solution.py:82
  45.8 0.6 dynamic_slice.65
  47.1 0.2 compare_and_fusion.4
  47.3 0.7 fusion.82
  48.1 0.8 fusion.83
  49.0 0.6 dynamic_slice.65
  50.2 0.2 compare_and_fusion.4
  50.5 0.7 fusion.82
  51.2 0.8 fusion.83
  52.1 0.6 dynamic_slice.65
  53.6 0.7 fusion.82
  54.4 0.8 fusion.83
  55.3 0.6 dynamic_slice.65
  56.7 0.7 fusion.82
  57.5 0.8 fusion.83
  58.4 43.4 %all_gather.10 = bf16[1,2048,128]{2,1,0:T(8,128)(2,1)S(1)} all-gather(bf16[1,128,128]{2,1,0:T(8,128)(2,1)S(1)} %copy-done.3), channel_id=1, replica_groups=mesh['dp'=1,'context'=16,'tensor'=2] {'context'}, dimensions={1}, use_global_device_ids=true | all-gather | bytes 557056 | tf_op jit(solution)/shard_map/all_gather | solution.py:38
  101.8 1.4 gather_fusion.1
  103.2 1.1 copy.68
  104.4 1.0 copy.44
  105.5 0.4 fusion.57
  105.9 32.2 %while.27 = (s32[]{:T(128)}, f32[1,128,16,128]{1,3,2,0:T(8,128)S(1)}, f32[4,1,512,256]{3,2,0,1:T(8,128)}, s32[4]{0:T(128)S(1)}, bf16[1,2048,128]{2,1,0:T(8,128)(...) while((s32[]{:T(128)}, ...), condition=%wide.region_8.9_spmd.clone, body=%wide.region_7.8_spmd.clone.sunk | while | flops 1353581056 | bytes 29461788 | solution.py:118
  106.0 0.7 dynamic_slice.70
  107.6 0.7 fusion.94
  108.3 0.9 fusion.97
  109.2 2.2 fusion.95
  111.5 0.8 fusion.98
  112.3 0.6 fusion.96
  113.2 0.8 constant_dynamic-update-slice_fusion.2
  114.0 0.7 dynamic_slice.70
  115.6 0.7 fusion.94
  116.3 1.0 fusion.97
  117.3 2.2 fusion.95
  119.5 0.8 fusion.98
  120.3 0.6 fusion.96
  121.2 0.9 constant_dynamic-update-slice_fusion.2
  122.1 0.7 dynamic_slice.70
  123.7 0.7 fusion.94
  124.4 0.9 fusion.97
  125.3 2.2 fusion.95
  127.5 0.8 fusion.98
  128.4 0.6 fusion.96
  129.2 0.8 constant_dynamic-update-slice_fusion.2
  130.1 0.7 dynamic_slice.70
  131.7 0.7 fusion.94
  132.4 1.0 fusion.97
  133.3 2.2 fusion.95
  135.6 0.8 fusion.98
  136.4 0.6 fusion.96
  137.3 0.9 constant_dynamic-update-slice_fusion.2
  138.1 3.6 gather_fusion.2
  141.9 74.7 %reduce-scatter.3.cloned.1.call-done = f32[1,128,256]{2,1,0:T(8,128)} async-done(((f32[1,2048,256]{2,1,0:T(8,128)}), f32[1,128,256]{2,1,0:T(8,128)}) %reduce-scatter.3.cloned.1.call-update) | async-done | bytes 131088 | tf_op jit(solution)/shard_map/reduce_scatter | solution.py:126
  216.6 10.3 %convolution_bitcast_fusion = f32[16384,256]{0,1:T(8,128)} fusion(bf16[1,128,16384]{2,1,0:T(8,128)(2,1)} %all-gather.2.cloned.1.call-done, f32[1,128,256]{2,1,0:T(8,128)} %reduce-scatter.3.cloned.1.call-done), kind=kOutput, calls=%fused_computation.61 | convolution fusion | flops 1073774592 | bytes 21102592 | tf_op jit(solution)/shard_map/bnd,bne->de/dot_general | solution.py:130
  227.1 1.0 copy.63
  228.1 357.5 %reduce-scatter.5.cloned.1.call-done = f32[1024,256]{0,1:T(8,128)} async-done(((f32[16384,256]{0,1:T(8,128)}), f32[1024,256]{0,1:T(8,128)}) %reduce-scatter.5.cloned.1.call-update) | async-done | bytes 1048592 | tf_op jit(solution)/shard_map/reduce_scatter | solution.py:129
  585.6 1.3 fusion.64
  586.8 1.0 copy.48
  587.8 1.0 copy.47
  (84 shorter events, 3.1 us)
Async XLA Ops:
  8.0 4.0 copy-start.2
  8.0 37.0 %copy-start.4 = (s32[1,16]{1,0:T(1,128)S(1)}, s32[1,16]{1,0:T(1,128)}, u32[]{:S(2)}) copy-start(s32[1,16]{1,0:T(1,128)} %param.18) | copy-start | bytes 196
  8.0 133.8 %all-gather.2.cloned.1.call-start = ((), (), s32[]{:S(2)}) async-start(), calls=%async_computation.3 | async-start | bytes 6291456 | tf_op jit(solution)/shard_map/all_gather | solution.py:128
  8.8 207.8 %reduce-scatter.3.cloned.1.call-start = ((), (), s32[]{:S(2)}) async-start(), calls=%async_computation.2 | async-start | bytes 2228224 | tf_op jit(solution)/shard_map/reduce_scatter | solution.py:126
  45.8 12.6 %copy-start.3 = (bf16[1,128,128]{2,1,0:T(8,128)(2,1)S(1)}, bf16[1,128,128]{2,1,0:T(8,128)(2,1)}, u32[]{:S(2)}) copy-start(bf16[1,128,128]{2,1,0:T(8,128)(2,1)} %param.14) | copy-start | bytes 98308
  45.8 58.5 %copy-start = (bf16[1,128,2048]{2,1,0:T(8,128)(2,1)S(1)}, bf16[1,128,2048]{2,1,0:T(8,128)(2,1)}, u32[]{:S(2)}) copy-start(bf16[1,128,2048]{2,1,0:T(8,128)(2,1)} %param.16) | copy-start | bytes 1572868
  105.9 32.2 %copy-start.5 = (s32[32]{0:T(128)S(1)}, s32[32]{0:T(128)}, u32[]{:S(2)}) copy-start(s32[32]{0:T(128)} %param.19) | copy-start | bytes 388
  106.0 2.3 copy-start.1
  114.0 2.3 copy-start.1
  122.1 2.3 copy-start.1
  130.1 2.3 copy-start.1
  141.8 443.8 %reduce-scatter.5.cloned.1.call-start = ((), (), s32[]{:S(2)}) async-start(), calls=%async_computation.4 | async-start | bytes 17825792 | tf_op jit(solution)/shard_map/reduce_scatter | solution.py:129
Sparse Core Ops, SparseCore 0:
  10.4 15.0 all-gather.1
Sparse Core Ops, SparseCore 1:
  141.9 74.7 reduce-scatter.2
  227.0 358.5 reduce-scatter.4
where the time goes:
time: 597 us; the launch traced here: 596 us
  waiting for transfers between devices  433 us (73%)
  blocking collectives  76.4 us (13%)
  matrix products  34.5 us (6%)
  local copies, waits for them, and re-layouts  23.2 us (4%)
  between operations  15.7 us (3%)
  other arithmetic  7.41 us (1%)
  loops' own time  6.07 us (1%)
    reduce_scatter x1, waiting for transfers between devices, on_device(): lax.psum_scatter(jnp.einsum('bnd,bne->de', token_rows, grads_low, preferr...  357 us
    reduce_scatter x1, waiting for transfers between devices, on_device(): lax.psum_scatter(stored_grads, 'context', scatter_dimension=1, tiled=True)  74.7 us
    all_gather x1, blocking collectives, on_device(): lax.all_gather(values, 'context', axis=1, tiled=True)  43.4 us
    all_gather x1, blocking collectives, on_device(): lax.all_gather(keys, 'context', axis=1, tiled=True)  33 us
  transfers between devices with their start and end apart: 3, of which 2 were waited for; matrix products, arithmetic and copies ran while one was open for 9% of the time, Pallas kernels for 0%

commit v1 on v0

--- a/solution.py
+++ b/solution.py
@@ -3,6 +3,24 @@
 import jax.numpy as jnp
 from jax import lax
 from jax.sharding import PartitionSpec as P
+
+
+def collect(array, axis, dim):
+    ways, here, hop = (lax.axis_size(axis), lax.axis_index(axis), array.shape[dim])
+    lengths = [n * ways if d == dim else n for d, n in enumerate(array.shape)]
+    full = lax.dynamic_update_slice_in_dim(
+        jnp.zeros(lengths, array.dtype), array, here * hop, axis=dim
+    )
+    going_up = going_down = array
+    for far in range(1, ways // 2 + 1):
+        going_up = lax.ppermute(going_up, axis, [(d, (d + 1) % ways) for d in range(ways)])
+        full = lax.dynamic_update_slice_in_dim(full, going_up, (here - far) % ways * hop, axis=dim)
+        if 2 * far < ways:
+            going_down = lax.ppermute(going_down, axis, [(d, (d - 1) % ways) for d in range(ways)])
+            full = lax.dynamic_update_slice_in_dim(
+                full, going_down, (here + far) % ways * hop, axis=dim
+            )
+    return full
 
 
 def table_lookup(entries, positions):
@@ -34,7 +52,7 @@
         jnp.where(span_slots[None, :] == slot_index[:, None], slot_index[None, :], 0), axis=1
     )
     gathered_keys, gathered_values = (
-        lax.all_gather(keys, "context", axis=1, tiled=True),
+        collect(keys, "context", 1),
         lax.all_gather(values, "context", axis=1, tiled=True),
     )
     key_rows = gathered_keys.reshape(batch_count, slot_count, span_rows, head_size)[

time: 597 us -> 616 us (1.032)
  blocking collectives: 76.4 us -> 35.4 us
  waiting for transfers between devices: 433 us -> 465 us
  starting transfers between devices: 0.12 us -> 26.2 us
    all_gather x1 -> x0, blocking collectives: 33 us -> none  [on_device(): lax.all_gather(keys, 'context', axis=1, tiled=True)]
    ppermute x0 -> x15, starting transfers between devices: none -> 25.9 us  [the longest x7 22.8 us: collect(): lax.ppermute(going_down, axis, [(d, (d - 1) % ways) for d in range(ways)])]
    ppermute x0 -> x15, waiting for transfers between devices: none -> 20.6 us  [the longest x8 14.5 us: collect(): lax.ppermute(going_up, axis, [(d, (d + 1) % ways) for d in range(ways)])]
    reduce_scatter x1, waiting for transfers between devices: 74.7 us -> 86.9 us  [on_device(): lax.psum_scatter(stored_grads, 'context', scatter_dimension=1, tiled=True)]
    all_gather x1, blocking collectives: 43.4 us -> 35.4 us  [on_device(): lax.all_gather(values, 'context', axis=1, tiled=True)]
  transfers between devices with their start and end apart: 3 -> 18, of which waited for: 2 -> 14; matrix products, arithmetic and copies ran while one was open for 9% -> 9% of each run, Pallas kernels for 0% -> 0%
where the time goes in v1:
time: 616 us
  waiting for transfers between devices  465 us (75%)
  blocking collectives  35.4 us (6%)
  matrix products  34.8 us (6%)
  starting transfers between devices  26.2 us (4%)
  local copies, waits for them, and re-layouts  23.6 us (4%)
  between operations  16 us (3%)
  other arithmetic  8.16 us (1%)
    reduce_scatter x1, waiting for transfers between devices, on_device(): lax.psum_scatter(jnp.einsum('bnd,bne->de', token_rows, grads_low, preferr...  358 us
    reduce_scatter x1, waiting for transfers between devices, on_device(): lax.psum_scatter(stored_grads, 'context', scatter_dimension=1, tiled=True)  86.9 us
    all_gather x1, blocking collectives, on_device(): lax.all_gather(values, 'context', axis=1, tiled=True)  35.4 us
    ppermute x7, starting transfers between devices, collect(): lax.ppermute(going_down, axis, [(d, (d - 1) % ways) for d in range(ways)])  22.8 us
    ppermute x8, waiting for transfers between devices, collect(): lax.ppermute(going_up, axis, [(d, (d + 1) % ways) for d in range(ways)])  14.5 us
  transfers between devices with their start and end apart: 18, of which 14 were waited for; matrix products, arithmetic and copies ran while one was open for 9% of the time, Pallas kernels for 0%

profile of v1, /device:TPU:10, one launch (start us, length us, event | category | flops | bytes accessed | tf_op | source)
XLA Modules:
  0.0 615.8 jit_solution(16565773617354535406)
XLA Ops:
  8.7 2.4 collective-permute-start
  11.1 0.8 select_reduce_fusion.1
  11.9 0.7 compare_select_fusion
  12.6 0.7 select_reduce_fusion
  13.4 35.4 %all_gather.6 = bf16[1,2048,128]{2,1,0:T(8,128)(2,1)S(1)} all-gather(bf16[1,128,128]{2,1,0:T(8,128)(2,1)} %param.14), channel_id=1, replica_groups=mesh['dp'=1,'context'=16,'tensor'=2] {'context'}, dimensions={1}, use_global_device_ids=true | all-gather | bytes 557056 | tf_op jit(solution)/shard_map/all_gather | solution.py:56
  48.8 1.1 copy.68
  49.9 1.1 copy.67
  51.9 1.0 copy.44
  53.6 1.4 gather_fusion.1
  55.0 5.4 collective-permute-start.3
  60.5 1.6 collective-permute-done.3
  62.0 2.3 collective-permute-start.5
  64.4 0.7 collective-permute-done.2
  65.6 1.2 collective-permute-done.5
  66.8 2.5 collective-permute-start.7
  69.4 0.9 collective-permute-done.4
  70.4 1.2 collective-permute-done.7
  71.7 3.6 collective-permute-start.9
  75.9 1.0 collective-permute-done.9
  76.9 4.2 collective-permute-start.11
  81.6 1.0 collective-permute-done.11
  82.7 4.1 collective-permute-start.13
  87.3 5.7 collective-permute-done.12
  93.1 5.7 collective-permute-done.14
  99.5 13.0 %while.26 = (s32[]{:T(128)}, f32[1,16,128]{2,1,0:T(8,128)S(1)}, f32[1,16,128]{2,1,0:T(8,128)S(1)}, s32[4]{0:T(128)S(1)}, s32[128]{0:T(128)S(1)}, /*index=5*/s32[...) while((s32[]{:T(128)}, f32[1,16,128]{2,1,0:T(8,128)S(1)}, ...), condition=%wide.region_6.7_spmd.clone, body=%wide.region_3.6_spmd.clone.sunk | while | flops 275982848 | bytes 9358550 | solution.py:100
  101.0 0.7 fusion.82
  101.8 0.9 fusion.83
  104.3 0.7 fusion.82
  105.0 0.9 fusion.83
  107.5 0.7 fusion.82
  108.3 0.9 fusion.83
  109.2 0.7 dynamic_slice.65
  110.8 0.7 fusion.82
  111.5 0.9 fusion.83
  112.5 32.4 %while.27 = (s32[]{:T(128)}, f32[1,128,16,128]{1,3,2,0:T(8,128)S(1)}, f32[4,1,512,256]{3,2,0,1:T(8,128)}, s32[4]{0:T(128)S(1)}, bf16[1,2048,128]{2,1,0:T(8,128)(...) while((s32[]{:T(128)}, ...), condition=%wide.region_8.9_spmd.clone, body=%wide.region_7.8_spmd.clone.sunk | while | flops 1353581056 | bytes 29461788 | solution.py:136
  112.5 0.7 dynamic_slice.70
  114.1 0.7 fusion.94
  114.8 1.0 fusion.97
  115.7 2.3 fusion.95
  118.0 0.8 fusion.98
  119.8 0.8 constant_dynamic-update-slice_fusion.18
  122.2 0.7 fusion.94
  122.9 1.0 fusion.97
  123.8 2.3 fusion.95
  126.1 0.8 fusion.98
  127.8 0.8 constant_dynamic-update-slice_fusion.18
  130.2 0.7 fusion.94
  130.9 1.0 fusion.97
  131.9 2.3 fusion.95
  134.2 0.8 fusion.98
  135.9 0.9 constant_dynamic-update-slice_fusion.18
  138.3 0.7 fusion.94
  139.1 1.0 fusion.97
  140.0 2.3 fusion.95
  142.3 0.8 fusion.98
  144.0 0.8 constant_dynamic-update-slice_fusion.18
  144.9 3.6 gather_fusion.2
  148.7 86.9 %reduce-scatter.3.cloned.1.call-done = f32[1,128,256]{2,1,0:T(8,128)} async-done(((f32[1,2048,256]{2,1,0:T(8,128)}), f32[1,128,256]{2,1,0:T(8,128)}) %reduce-scatter.3.cloned.1.call-update) | async-done | bytes 131088 | tf_op jit(solution)/shard_map/reduce_scatter | solution.py:144
  235.6 10.4 %convolution_bitcast_fusion = f32[16384,256]{0,1:T(8,128)} fusion(bf16[1,128,16384]{2,1,0:T(8,128)(2,1)} %all-gather.2.cloned.1.call-done, f32[1,128,256]{2,1,0:T(8,128)} %reduce-scatter.3.cloned.1.call-done), kind=kOutput, calls=%fused_computation.61 | convolution fusion | flops 1073774592 | bytes 21102592 | tf_op jit(solution)/shard_map/bnd,bne->de/dot_general | solution.py:148
  246.2 1.0 copy.63
  247.2 357.8 %reduce-scatter.5.cloned.1.call-done = f32[1024,256]{0,1:T(8,128)} async-done(((f32[16384,256]{0,1:T(8,128)}), f32[1024,256]{0,1:T(8,128)}) %reduce-scatter.5.cloned.1.call-update) | async-done | bytes 1048592 | tf_op jit(solution)/shard_map/reduce_scatter | solution.py:147
  605.0 1.3 fusion.64
  606.3 1.0 copy.48
  607.3 1.0 copy.47
  (128 shorter events, 14.7 us)
Async XLA Ops:
  8.0 43.6 %copy-start.3 = (bf16[1,128,128]{2,1,0:T(8,128)(2,1)S(1)}, bf16[1,128,128]{2,1,0:T(8,128)(2,1)}, u32[]{:S(2)}) copy-start(bf16[1,128,128]{2,1,0:T(8,128)(2,1)} %param.13) | copy-start | bytes 98308
  8.0 43.9 %copy-start = (bf16[1,128,2048]{2,1,0:T(8,128)(2,1)S(1)}, bf16[1,128,2048]{2,1,0:T(8,128)(2,1)}, u32[]{:S(2)}) copy-start(bf16[1,128,2048]{2,1,0:T(8,128)(2,1)} %param.16) | copy-start | bytes 1572868
  8.0 43.0 %copy-start.4 = (s32[1,16]{1,0:T(1,128)S(1)}, s32[1,16]{1,0:T(1,128)}, u32[]{:S(2)}) copy-start(s32[1,16]{1,0:T(1,128)} %param.18) | copy-start | bytes 196
  8.0 44.9 %copy-start.1 = (bf16[1,128,2048]{2,1,0:T(8,128)(2,1)S(1)}, bf16[1,128,2048]{2,1,0:T(8,128)(2,1)}, u32[]{:S(2)}) copy-start(bf16[1,128,2048]{2,1,0:T(8,128)(2,1)} %param.12) | copy-start | bytes 1572868
  8.0 140.7 %all-gather.2.cloned.1.call-start = ((), (), s32[]{:S(2)}) async-start(), calls=%async_computation.3 | async-start | bytes 6291456 | tf_op jit(solution)/shard_map/all_gather | solution.py:146
  8.1 46.9 %collective-permute-start.1 = (bf16[1,128,128]{2,1,0:T(8,128)(2,1)}, bf16[1,128,128]{2,1,0:T(8,128)(2,1)S(1)}, u32[]{:S(2)}, u32[]{:S(2)}) collective-permute-start(bf16[1,128,128]{2,1,0:T(8,128)(2,1)} %param.13), channel_id=1, source_target_pairs={{0,30},{2,0},{4,2},{6,4},{8,6},{10,8},{12,10},{14,12},{16,14},{18,... | collective-permute-start | bytes 98312 | tf_op jit(solution)/shard_map/ppermute | solution.py:19
  8.7 51.8 %collective-permute-start = (bf16[1,128,128]{2,1,0:T(8,128)(2,1)}, bf16[1,128,128]{2,1,0:T(8,128)(2,1)S(1)}, u32[]{:S(2)}, u32[]{:S(2)}) collective-permute-start(bf16[1,128,128]{2,1,0:T(8,128)(2,1)} %param.13), channel_id=1, source_target_pairs={{0,2},{2,4},{4,6},{6,8},{8,10},{10,12},{12,14},{14,16},{16,18},{18... | collective-permute-start | bytes 98312 | tf_op jit(solution)/shard_map/ppermute | solution.py:16
  11.1 224.5 %reduce-scatter.3.cloned.1.call-start = ((), (), s32[]{:S(2)}) async-start(), calls=%async_computation.2 | async-start | bytes 2228224 | tf_op jit(solution)/shard_map/reduce_scatter | solution.py:144
  55.0 7.0 %collective-permute-start.3 = (bf16[1,128,128]{2,1,0:T(8,128)(2,1)S(1)}, bf16[1,128,128]{2,1,0:T(8,128)(2,1)S(1)}, u32[]{:S(2)}, u32[]{:S(2)}) collective-permute-start(bf16[1,128,128]{2,1,0:T(8,128)(2,1)S(1)} %collective-permute-done.1), channel_id=1, source_target_pairs={{0,30},{2,0},{4,2},{6,4},{8,6},{10,8},{12,10},{14,12},{16,14},{18,... | collective-permute-start | bytes 98312 | tf_op jit(solution)/shard_map/ppermute | solution.py:19
  60.4 4.6 collective-permute-start.2
  62.0 4.8 collective-permute-start.5
  65.1 5.2 collective-permute-start.4
  66.8 4.8 collective-permute-start.7
  70.3 5.6 collective-permute-start.6
  71.7 5.2 collective-permute-start.9
  75.9 5.7 collective-permute-start.8
  76.9 5.8 collective-permute-start.11
  81.6 5.7 collective-permute-start.10
  82.7 10.4 %collective-permute-start.13 = (bf16[1,128,128]{2,1,0:T(8,128)(2,1)S(1)}, bf16[1,128,128]{2,1,0:T(8,128)(2,1)S(1)}, u32[]{:S(2)}, u32[]{:S(2)}) collective-permute-start(bf16[1,128,128]{2,1,0:T(8,128)(2,1)S(1)} %collective-permute-done.11), channel_id=1, source_target_pairs={{0,30},{2,0},{4,2},{6,4},{8,6},{10,8},{12,10},{14,12},{16,14},{18,... | collective-permute-start | bytes 98312 | tf_op jit(solution)/shard_map/ppermute | solution.py:19
  87.3 5.7 collective-permute-start.12
  93.0 5.7 collective-permute-start.14
  112.5 2.3 copy-start.2
  120.6 2.3 copy-start.2
  128.7 2.3 copy-start.2
  136.8 2.3 copy-start.2
  148.5 456.5 %reduce-scatter.5.cloned.1.call-start = ((), (), s32[]{:S(2)}) async-start(), calls=%async_computation.4 | async-start | bytes 17825792 | tf_op jit(solution)/shard_map/reduce_scatter | solution.py:147
Sparse Core Ops, SparseCore 0:
  11.2 17.7 all-gather.1
Sparse Core Ops, SparseCore 1:
  148.6 87.0 reduce-scatter.2
  246.1 358.9 reduce-scatter.4
